TPU v7x, 32 devices: a whole 2x2x4 slice. The times are simulated.
32 devices in a mesh: lat: 8 (over z, core), lon: 4 (over y, x).
Axes of the slice: x: 2, y: 2, z: 4, core: 2. Of those that a mesh axis runs over, the one named last changes fastest.
Arguments:
- predicted_state: float32 [1440, 13312], P('lon', 'lat'), may hold values from -24 to 24
- verified_state: float32 [1440, 13312], P('lon', 'lat'), may hold values from -20 to 20
- normal_state: float32 [1440, 13312], P('lon', 'lat'), may hold values from -3 to 3
Outputs:
- energy_curves: float32 [3, 52, 721], replicated
- rms_error: float32 [52], replicated
- anomaly_corr: float32 [52], replicated
All inputs are finite; a program needn't handle non-finite values.
Results may differ from a plain program's by a relative error of at most 0.00005.
Values sent between devices are 32-bit elements; how exact they have to be, the bound alone decides.
A program may use at most 64 MiB of HBM per device.

v0:
```python
import jax
import jax.numpy as jnp
from jax import lax
from jax.sharding import PartitionSpec as P

FIELDS = 52


epsilon = 1e-06


def latitude_weights(lat_index, parallel_number):
    return jnp.cos(jnp.pi * ((lat_index.astype(jnp.float32) + 0.5) / parallel_number - 0.5))


def dft_table(lon_rows, lon_total, wave_count):
    longitudes = jnp.arange(lon_rows, dtype=jnp.int32)
    waves = jnp.arange(wave_count, dtype=jnp.int32)
    phase = longitudes[:, None] * waves[None, :] % lon_total
    angle = 2.0 * jnp.pi / lon_total * phase.astype(jnp.float32)
    return jnp.concatenate([jnp.cos(angle), -jnp.sin(angle)], axis=1)


def transform_columns(stacked, table):
    return lax.dot_general(
        stacked,
        table,
        (((0,), (0,)), ((), ())),
        precision=lax.Precision.HIGHEST,
        preferred_element_type=jnp.float32,
    )


def row_powers(fore_coeffs, true_coeffs, wave_count):
    diff_coeffs = fore_coeffs - true_coeffs

    def square(coeffs):
        return (
            coeffs[:, :wave_count] * coeffs[:, :wave_count]
            + coeffs[:, wave_count:] * coeffs[:, wave_count:]
        )

    return jnp.stack([square(fore_coeffs), square(true_coeffs), square(diff_coeffs)], axis=1)


def local(predicted_state, verified_state, normal_state):
    quantity_labels = FIELDS
    meridian_lines, meridian_number = predicted_state.shape
    parallel_lines = meridian_number // quantity_labels
    parallel_number = parallel_lines * lax.axis_size("lat")
    lon_devices = lax.axis_size("lon")
    lon_total = meridian_lines * lon_devices
    wave_count = lon_total // 2 + 1
    row_share = meridian_number // lon_devices
    lat_first = lax.axis_index("lat") * parallel_lines
    weights = latitude_weights(
        lat_first + jnp.arange(parallel_lines, dtype=jnp.int32), parallel_number
    )
    weight_total = jnp.sum(
        latitude_weights(jnp.arange(parallel_number, dtype=jnp.int32), parallel_number)
    )
    predicted_block = predicted_state.reshape(meridian_lines, parallel_lines, quantity_labels)
    observed_block = verified_state.reshape(meridian_lines, parallel_lines, quantity_labels)
    normal_block = normal_state.reshape(meridian_lines, parallel_lines, quantity_labels)
    mismatch_parts = predicted_block - observed_block
    predicted_anomalies = predicted_block - normal_block
    observed_anomalies = observed_block - normal_block
    broad_layout = weights[None, :, None]
    skill_terms = jnp.stack(
        [
            jnp.sum(broad_layout * mismatch_parts * mismatch_parts, axis=(0, 1)),
            jnp.sum(broad_layout * predicted_anomalies * observed_anomalies, axis=(0, 1)),
            jnp.sum(broad_layout * predicted_anomalies * predicted_anomalies, axis=(0, 1)),
            jnp.sum(broad_layout * observed_anomalies * observed_anomalies, axis=(0, 1)),
        ]
    )
    predicted_meridians = predicted_block.transpose(0, 2, 1).reshape(
        meridian_lines, meridian_number
    )
    true_cols = observed_block.transpose(0, 2, 1).reshape(meridian_lines, meridian_number)
    full_table = dft_table(lon_total, lon_total, wave_count)
    fore_blocks = predicted_meridians.reshape(meridian_lines, lon_devices, row_share)
    true_blocks = true_cols.reshape(meridian_lines, lon_devices, row_share)
    fore_part = lax.all_to_all(fore_blocks, "lon", split_axis=1, concat_axis=0, tiled=True)[:, 0, :]
    true_part = lax.all_to_all(true_blocks, "lon", split_axis=1, concat_axis=0, tiled=True)[:, 0, :]
    items = fore_part.shape[1]
    stacked = jnp.concatenate([fore_part, true_part], axis=1)
    coeffs = transform_columns(stacked, full_table)
    powers = row_powers(coeffs[:items], coeffs[items:], wave_count)
    share_start = lax.axis_index("lon") * row_share
    global_cols = share_start + jnp.arange(row_share, dtype=jnp.int32)
    field_of = global_cols // parallel_lines
    row_weights = latitude_weights(lat_first + global_cols % parallel_lines, parallel_number)
    row_scale = row_weights / (lon_total * lon_total * weight_total)
    weighted = powers.reshape(row_share, 3 * wave_count) * row_scale[:, None]
    field_index = jnp.arange(quantity_labels, dtype=jnp.int32)
    window = min(quantity_labels, row_share // parallel_lines + 2)
    first_field = share_start // parallel_lines
    window_index = jnp.arange(window, dtype=jnp.int32)
    offset = field_of - first_field
    selector = (offset[None, :] == window_index[:, None]).astype(jnp.float32)
    band_sum = jnp.dot(
        selector, weighted, precision=lax.Precision.HIGHEST, preferred_element_type=jnp.float32
    )
    band_sum = lax.psum(band_sum, "lat")
    gathered = lax.all_gather(band_sum, "lon", axis=0, tiled=True)
    slot_index = jnp.arange(lon_devices * window, dtype=jnp.int32)
    slot_field = slot_index // window * row_share // parallel_lines + slot_index % window
    placer = (slot_field[None, :] == field_index[:, None]).astype(jnp.float32)
    summed = jnp.dot(
        placer, gathered, precision=lax.Precision.HIGHEST, preferred_element_type=jnp.float32
    )
    energy_curves = summed.reshape(quantity_labels, 3, wave_count).transpose(1, 0, 2)
    skill_means = lax.psum(skill_terms, ("lat", "lon")) / (lon_total * weight_total)
    rms_error = jnp.sqrt(skill_means[0])
    anomaly_corr = skill_means[1] / jnp.sqrt(
        (skill_means[2] + epsilon) * (skill_means[3] + epsilon)
    )
    return (energy_curves, rms_error, anomaly_corr)


def solution(mesh):
    in_specs = (P("lon", "lat"), P("lon", "lat"), P("lon", "lat"))
    out_specs = (P(), P(), P())
    return jax.shard_map(local, mesh=mesh, in_specs=in_specs, out_specs=out_specs, check_vma=False)
```

profile of v0, /device:TPU:0, one launch (start us, length us, event | category | flops | bytes accessed | tf_op | source)
XLA Modules:
  0.0 274.7 jit_solution(18060614692774121550)
XLA Ops:
  7.2 3.2 %copy.26 = f32[360,1664]{0,1:T(8,128)} copy(f32[360,1664]{1,0:T(8,128)} %param.4) | data formatting | bytes 4792320 | tf_op args[1]
  10.4 2.4 reshape.125
  12.8 1.9 copy.27
  14.8 5.3 %all-to-all-start.1 = ((f32[360,4,416]{0,2,1:T(8,128)}), f32[360,4,416]{0,2,1:T(8,128)}, u32[]{:S(2)}, u32[]{:S(2)}) async-start(f32[360,4,416]{0,2,1:T(8,128)} %bitcast.41), calls=%async_computation.1 | async-start | bytes 5111808 | tf_op jit(solution)/shard_map/all_to_all | solution.py:85
  20.1 2.1 copy.23
  22.2 2.4 reshape.124
  24.7 2.1 copy.24
  27.0 23.8 %all-to-all-done.1 = f32[360,4,416]{0,2,1:T(8,128)} async-done(((f32[360,4,416]{0,2,1:T(8,128)}), f32[360,4,416]{0,2,1:T(8,128)}, u32[]{:S(2)}, u32[]{:S(2)}) %all-to-all-start.1) | async-done | bytes 2396192 | tf_op jit(solution)/shard_map/all_to_all | solution.py:85
  50.8 3.6 %all-to-all-start = ((f32[360,4,416]{0,2,1:T(8,128)}), f32[360,4,416]{0,2,1:T(8,128)S(1)}, u32[]{:S(2)}, u32[]{:S(2)}) async-start(f32[360,4,416]{0,2,1:T(8,128)} %bitcast.39), calls=%async_computation | async-start | bytes 5111808 | tf_op jit(solution)/shard_map/all_to_all | solution.py:84
  54.5 4.3 %fusion.17 = (f32[1664]{0:T(1024)S(1)}, f32[1664]{0:T(1024)S(1)}, f32[1664]{0:T(1024)S(1)}, f32[1664]{0:T(1024)S(1)}) fusion(f32[360,1664]{1,0:T(8,128)} %param.3, f32[360,1664]{1,0:T(8,128)} %param.4, f32[1664]{0:T(1024)S(1)} %mul.171, f32[360,1664]{1,0:T(8,128)} %param.5), kind=kLoop, calls=%fused_computation.26 | loop fusion | flops 8379904 | bytes 7221760 | tf_op jit(solution)/shard_map/reduce_sum | solution.py:71
  61.3 57.3 %psum.15 = f32[4,52]{1,0:T(4,128)S(1)} all-reduce(f32[4,52]{1,0:T(4,128)S(1)} %pad_maximum_fusion.1), channel_id=1, replica_groups=mesh['lat'=8,'lon'=4] {'lat','lon'}, use_global_device_ids=true, to_apply=%region_10.11 | all-reduce | flops 208 | bytes 1664 | tf_op jit(solution)/shard_map/psum | solution.py:114
  119.2 19.7 %sine_negate_fusion = (f32[1440,721]{1,0:T(8,128)}, f32[1440,721]{1,0:T(8,128)}) fusion(), kind=kLoop, calls=%fused_computation.12 | loop fusion | flops 10382400 | bytes 8305920 | tf_op jit(solution)/shard_map/neg | solution.py:21
  138.9 4.8 %copy.28 = f32[4,360,1,416]{1,0,3,2:T(4,128)} copy(f32[4,360,1,416]{1,3,0,2:T(8,128)} %bitcast.7) | data formatting | bytes 4792320 | tf_op jit(solution)/shard_map/all_to_all | solution.py:85
  143.7 4.0 %squeeze.5 = f32[1440,416]{0,1:T(8,128)} reshape(f32[4,360,1,416]{1,0,3,2:T(4,128)} %copy.28) | data formatting | bytes 4792320 | tf_op jit(solution)/shard_map/squeeze | solution.py:85
  147.7 3.1 %copy.25 = f32[4,360,1,416]{1,0,3,2:T(4,128)} copy(f32[4,360,1,416]{1,3,0,2:T(8,128)S(1)} %bitcast.40) | data formatting | bytes 4792320 | tf_op jit(solution)/shard_map/all_to_all | solution.py:84
  150.8 4.2 %squeeze.4 = f32[1440,416]{0,1:T(8,128)} reshape(f32[4,360,1,416]{1,0,3,2:T(4,128)} %copy.25) | data formatting | bytes 4792320 | tf_op jit(solution)/shard_map/squeeze | solution.py:84
  155.0 29.4 %fusion = f32[832,1442]{1,0:T(8,128)S(1)} fusion(f32[1440,721]{1,0:T(8,128)} %get-tuple-element.20, f32[1440,721]{1,0:T(8,128)} %get-tuple-element.21, f32[1440,416]{0,1:T(8,128)S(1)} %copy-done.1, f32[1440,416]{0,1:T(8,128)} %squeeze.4), kind=kOutput, calls=%fused_computation | convolution fusion | flops 20734851072 | bytes 17897216 | tf_op jit(solution)/shard_map/dot_general | solution.py:25
  186.0 2.1 pad_maximum_fusion
  188.1 5.6 %copy.29 = f32[416,3,721]{0,2,1:T(8,128)} copy(f32[416,3,721]{2,0,1:T(8,128)} %pad_maximum_fusion) | data formatting | bytes 7198464 | tf_op jit(solution)/shard_map/stack | solution.py:43
  193.7 4.9 %reshape.126 = f32[416,2163]{0,1:T(8,128)} reshape(f32[416,3,721]{0,2,1:T(8,128)} %copy.29) | data formatting | bytes 7198464 | tf_op jit(solution)/shard_map/reshape | solution.py:95
  198.6 5.2 %fusion.7 = f32[15,2163]{1,0:T(8,128)} fusion(f32[416,2163]{0,1:T(8,128)} %reshape.126, f32[416]{0:T(512)S(1)} %fusion.37, s32[416]{0:T(512)S(1)} %fusion.29), kind=kOutput, calls=%fused_computation.8 | convolution fusion | flops 162871488 | bytes 3732340 | tf_op jit(solution)/shard_map/dot_general | solution.py:102
  203.8 51.8 %all-reduce.2.cloned.1.call-done = f32[15,2163]{1,0:T(8,128)} async-done(((f32[15,2163]{1,0:T(8,128)}), f32[15,2163]{1,0:T(8,128)}) %all-reduce.2.cloned.1.call-update) | async-done | bytes 129796 | tf_op jit(solution)/shard_map/psum | solution.py:105
  255.6 10.4 %all-gather = f32[4,15,2163]{2,1,0:T(8,128)S(1)} all-gather(f32[1,15,2163]{2,1,0:T(8,128)} %bitcast.43), channel_id=1, replica_groups=mesh['lat'=8,'lon'=4] {'lon'}, dimensions={0}, use_global_device_ids=true | all-gather | bytes 648900 | tf_op jit(solution)/shard_map/all_gather | solution.py:106
  267.0 0.9 copy.30
  (31 shorter events, 4.5 us)
Async XLA Ops:
  14.8 5.3 %copy-start = (f32[360,1664]{1,0:T(8,128)S(1)}, f32[360,1664]{1,0:T(8,128)}, u32[]{:S(2)}) copy-start(f32[360,1664]{1,0:T(8,128)} %param.3) | copy-start | bytes 7188484
  14.8 36.1 %all-to-all-start.1 = ((f32[360,4,416]{0,2,1:T(8,128)}), f32[360,4,416]{0,2,1:T(8,128)}, u32[]{:S(2)}, u32[]{:S(2)}) async-start(f32[360,4,416]{0,2,1:T(8,128)} %bitcast.41), calls=%async_computation.1 | async-start | bytes 5111808 | tf_op jit(solution)/shard_map/all_to_all | solution.py:85
  50.8 96.9 %all-to-all-start = ((f32[360,4,416]{0,2,1:T(8,128)}), f32[360,4,416]{0,2,1:T(8,128)S(1)}, u32[]{:S(2)}, u32[]{:S(2)}) async-start(f32[360,4,416]{0,2,1:T(8,128)} %bitcast.39), calls=%async_computation | async-start | bytes 5111808 | tf_op jit(solution)/shard_map/all_to_all | solution.py:84
  54.5 201.1 %all-reduce.2.cloned.1.call-start = ((), (), s32[]{:S(2)}) async-start(), calls=%async_computation.2 | async-start | bytes 278528 | tf_op jit(solution)/shard_map/psum | solution.py:105
  150.8 4.2 %copy-start.1 = (f32[1440,416]{0,1:T(8,128)S(1)}, f32[1440,416]{0,1:T(8,128)}, u32[]{:S(2)}) copy-start(f32[1440,416]{0,1:T(8,128)} %squeeze.5) | copy-start | bytes 7188484
Sparse Core Ops, SparseCore 0:
  203.9 51.6 all-reduce.1
where the time goes:
time: 276 us; the launch traced here: 275 us
  waiting for transfers between devices  75.7 us (27%)
  blocking collectives  67.7 us (25%)
  local copies, waits for them, and re-layouts  42.8 us (16%)
  matrix products  35 us (13%)
  other arithmetic  29 us (11%)
  between operations  15.5 us (6%)
  starting transfers between devices  9.01 us (3%)
    psum x1, blocking collectives, local(): lax.psum(skill_terms, ('lat', 'lon')) / (lon_total * weight_total)  57.3 us
    psum x1, waiting for transfers between devices, local(): band_sum = lax.psum(band_sum, 'lat')  51.8 us
    dot_general x1, matrix products, transform_columns(): lax.dot_general(stacked, table, (((0,), (0,)), ((), ())), precision=lax.P...  29.4 us
    all_to_all x1, waiting for transfers between devices, local(): lax.all_to_all(true_blocks, 'lon', split_axis=1, concat_axis=0, tiled=True)  23.8 us
    neg x1, other arithmetic, dft_table(): return jnp.concatenate([jnp.cos(angle), -jnp.sin(angle)], axis=1)  19.7 us
    all_gather x1, blocking collectives, local(): gathered = lax.all_gather(band_sum, 'lon', axis=0, tiled=True)  10.4 us
    unnamed x8, local copies, waits for them, and re-layouts  6.32 us
    another operation x1, local copies, waits for them, and re-layouts, row_powers(): jnp.stack([square(fore_coeffs), square(true_coeffs), square(diff_coeffs)]...  5.61 us
  transfers between devices with their start and end apart: 3, of which 2 were waited for; matrix products, arithmetic and copies ran while one was open for 15% of the time, Pallas kernels for 0%

commit v1 on v0

--- a/solution.py
+++ b/solution.py
@@ -1,9 +1,16 @@
+import functools
+
 import jax
 import jax.numpy as jnp
+import numpy as np
 from jax import lax
+from jax.experimental import pallas as pl
+from jax.experimental.pallas import tpu as pltpu
 from jax.sharding import PartitionSpec as P
 
 FIELDS = 52
+LANES = 128
+MESH = pl.DeviceIdType.MESH
 
 
 epsilon = 1e-06
@@ -119,7 +126,373 @@
     return (energy_curves, rms_error, anomaly_corr)
 
 
+def split_np(values):
+    hi = values.astype(jnp.bfloat16)
+    lo = (values - hi.astype(np.float64)).astype(jnp.bfloat16)
+    return hi, lo
+
+
+def plan_constants(rows, cols, lat_devices, lon_devices):
+    total = rows * lon_devices
+    waves = total // 2 + 1
+    depth = -(-rows // LANES) * LANES
+    per_class = -(-(-(-waves // 4)) // 8) * 8
+    table = np.zeros((4, 2 * per_class, depth), np.float64)
+    lons = np.arange(rows)
+    for r in range(4):
+        k = np.arange(r, waves, 4)
+        angle = 2.0 * np.pi * ((k[:, None] * lons[None, :]) % total) / total
+        table[r, : len(k), :rows] = np.cos(angle)
+        table[r, per_class : per_class + len(k), :rows] = np.sin(angle)
+    hi, lo = split_np(table)
+    lat_lines = cols // FIELDS
+    lat_total = lat_lines * lat_devices
+    all_weights = np.cos(np.pi * ((np.arange(lat_total) + 0.5) / lat_total - 0.5))
+    scale = 1.0 / (float(total) * float(total) * all_weights.sum())
+    tiles = cols // LANES
+    piece = LANES // lon_devices
+    slots = tiles + lon_devices
+    col_of = np.full((slots, LANES), -1, np.int64)
+    for t in range(tiles):
+        col_of[t] = np.arange(LANES) + LANES * t
+    for d in range(lon_devices):
+        col_of[tiles + d, :piece] = (tiles - 1) * LANES + piece * d + np.arange(piece)
+    valid = col_of >= 0
+    field = np.where(valid, col_of % FIELDS, -1).astype(np.int32)
+    weight = np.zeros((lat_devices, slots, LANES), np.float64)
+    for a in range(lat_devices):
+        weight[a] = np.where(valid, all_weights[a * lat_lines + np.maximum(col_of, 0) // FIELDS] * scale, 0.0)
+    return hi, lo, field, weight.reshape(lat_devices * slots, LANES).astype(np.float32)
+
+
+def kernel(
+    dims, fore, true, norm, tab_hi, tab_lo, field, weight,
+    energy, skill,
+    fb, tb, nb, rx, ps, pr, bhi, blo, pbuf, acc, r0, half, r1, quart, r2, full,
+    load_sem, own_sem, xs, xr, qs, qr, ss, sr,
+):
+    rows, cols, n_lat, n_lon, total = dims
+    n_z = n_lat // 2
+    lat = lax.axis_index("lat")
+    lon = lax.axis_index("lon")
+    core = lat % 2
+    z = lat // 2
+    tiles = cols // LANES
+    own_tiles = tiles // n_lon
+    slots = tiles + n_lon
+    piece = LANES // n_lon
+    depth = tab_hi.shape[2]
+    per_class = tab_hi.shape[1] // 2
+    waves = total // 2 + 1
+    n_rows = 3 * FIELDS + 4
+    sibling = {"lat": lat + 1 - 2 * core, "lon": lon}
+
+    def lon_peer(p):
+        return {"lat": lat, "lon": (lon + p) % n_lon}
+
+    def z_peer(p):
+        return {"lat": (z + p) % n_z * 2 + core, "lon": lon}
+
+    barrier = pltpu.get_barrier_semaphore()
+    peers = [sibling] + [lon_peer(p) for p in range(1, n_lon)] + [z_peer(p) for p in range(1, n_z)]
+    for d in peers:
+        pl.semaphore_signal(barrier, inc=1, device_id=d, device_id_type=MESH)
+    loads = [
+        pltpu.make_async_copy(src, dst, load_sem.at[i])
+        for i, (src, dst) in enumerate(((fore, fb), (true, tb), (norm, nb)))
+    ]
+    for c in loads:
+        c.start()
+    sources = (fore, true)
+
+    def tile_ref(a, t):
+        return sources[a].at[:, pl.ds(pl.multiple_of(t * LANES, LANES), LANES)]
+
+    own = {}
+    for c in range(own_tiles):
+        for a in range(2):
+            own[a, c] = pltpu.make_async_copy(
+                tile_ref(a, lon * own_tiles + c), rx.at[a, c, lon], own_sem.at[a, c]
+            )
+            own[a, c].start()
+    pl.semaphore_wait(barrier, len(peers))
+
+    sends = {}
+
+    def send_tile(c):
+        for p in (2, 1, 3) if n_lon == 4 else range(1, n_lon):
+            for a in range(2):
+                dest = (lon + p) % n_lon
+                sends[a, c, p] = pltpu.make_async_remote_copy(
+                    src_ref=tile_ref(a, dest * own_tiles + c),
+                    dst_ref=rx.at[a, c, lon],
+                    send_sem=xs.at[a, c, p - 1],
+                    recv_sem=xr.at[a, c, p - 1],
+                    device_id=lon_peer(p),
+                    device_id_type=MESH,
+                )
+                sends[a, c, p].start()
+
+    send_tile(0)
+    loads[0].wait()
+    loads[1].wait()
+    last = (tiles - 1) * LANES
+    pad = jnp.zeros((depth - rows, LANES), jnp.float32)
+    for a, block in enumerate((fb, tb)):
+        flipped = jnp.concatenate([block[:, last : last + LANES], pad], axis=0).T
+        ps[a] = flipped.reshape(n_lon, piece, depth)
+    for c in range(1, own_tiles):
+        send_tile(c) if c == 1 else None
+    for p in range(1, n_lon):
+        for a in range(2):
+            sends[a, "piece", p] = pltpu.make_async_remote_copy(
+                src_ref=ps.at[a, (lon + p) % n_lon],
+                dst_ref=pr.at[a, lon],
+                send_sem=qs.at[a, p - 1],
+                recv_sem=qr.at[a, p - 1],
+                device_id=lon_peer(p),
+                device_id_type=MESH,
+            )
+            sends[a, "piece", p].start()
+    for c in range(2, own_tiles):
+        send_tile(c)
+
+    acc[...] = jnp.zeros_like(acc)
+    pbuf[...] = jnp.zeros_like(pbuf)
+    loads[2].wait()
+    field_rows = lax.broadcasted_iota(jnp.int32, (LANES, LANES), 0)
+
+    def skill_tile(t, carry):
+        lanes = pl.ds(pl.multiple_of(t * LANES, LANES), LANES)
+        f, v, n = fb[:, lanes], tb[:, lanes], nb[:, lanes]
+        e, af, at = f - v, f - n, v - n
+
+        def total_of(u):
+            return jnp.sum(u, axis=0, keepdims=True)
+
+        sums = jnp.concatenate(
+            [jnp.zeros((4, LANES), jnp.float32), total_of(e * e), total_of(af * at), total_of(af * af), total_of(at * at)],
+            axis=0,
+        )
+        sums = sums * (weight[pl.ds(lat * slots + t, 1), :] * float(total))
+        pick = (field_rows == field[pl.ds(t, 1), :]).astype(jnp.float32)
+        return carry + lax.dot_general(
+            sums, pick, (((1,), (1,)), ((), ())),
+            precision=lax.Precision.HIGHEST, preferred_element_type=jnp.float32,
+        )
+
+    skill_sums = lax.fori_loop(0, tiles, skill_tile, jnp.zeros((8, LANES), jnp.float32))
+    acc[n_rows - 8 : n_rows, :] = skill_sums
+
+    out_rows = lax.broadcasted_iota(jnp.int32, (n_rows, LANES), 0)
+
+    def put(group, a, y):
+        y = jnp.concatenate([y, pad], axis=0)
+        hi = y.astype(jnp.bfloat16)
+        lo = (y - hi.astype(jnp.float32)).astype(jnp.bfloat16)
+        at = group * 2 * LANES + a * LANES
+        bhi[:, at : at + LANES] = hi
+        blo[:, at : at + LANES] = lo
+
+    def product(r, start, width):
+        cut = slice(start, start + width)
+        th, tl = tab_hi[r], tab_lo[r]
+        return (
+            jnp.dot(th, bhi[:, cut], preferred_element_type=jnp.float32)
+            + jnp.dot(th, blo[:, cut], preferred_element_type=jnp.float32)
+            + jnp.dot(tl, bhi[:, cut], preferred_element_type=jnp.float32)
+        )
+
+    def process(c, slot):
+        for a in range(2):
+            x = [rx[a, c, q] for q in range(4)]
+            s02, s13 = x[0] + x[2], x[1] + x[3]
+            put(0, a, s02 + s13)
+            put(1, a, s02 - s13)
+            put(2, a, x[0] - x[2])
+            put(3, a, x[1] - x[3])
+        w = weight[pl.ds(lat * slots + slot, 1), :]
+        for r in range(4):
+            if r % 2 == 0:
+                both = product(r, (r // 2) * 2 * LANES, 2 * LANES)
+                re, im = both[:per_class], both[per_class:]
+            else:
+                both = product(r, 4 * LANES, 4 * LANES)
+                u, v = both[:per_class], both[per_class:]
+                g = 1.0 if r == 1 else -1.0
+                re = u[:, : 2 * LANES] - g * v[:, 2 * LANES :]
+                im = v[:, : 2 * LANES] + g * u[:, 2 * LANES :]
+            for curve in range(3):
+                if curve == 2:
+                    a, b = re[:, :LANES] - re[:, LANES:], im[:, :LANES] - im[:, LANES:]
+                else:
+                    cut = slice(curve * LANES, (curve + 1) * LANES)
+                    a, b = re[:, cut], im[:, cut]
+                pbuf.at[curve][pl.ds(r, per_class, stride=4), :] = (a * a + b * b) * w
+        fld = field[pl.ds(slot, 1), :]
+        for curve in range(3):
+            power = pbuf[curve]
+            hi = power.astype(jnp.bfloat16)
+            lo = (power - hi.astype(jnp.float32)).astype(jnp.bfloat16)
+            pick = (out_rows == jnp.where(fld >= 0, fld + FIELDS * curve, -1)).astype(jnp.float32).astype(jnp.bfloat16)
+            part = lax.dot_general(
+                jnp.concatenate([pick, pick], axis=1), jnp.concatenate([hi, lo], axis=1),
+                (((1,), (1,)), ((), ())), preferred_element_type=jnp.float32,
+            )
+            for t in range(part.shape[1] // LANES):
+                acc[t * n_rows : (t + 1) * n_rows, :] += part[:, t * LANES : (t + 1) * LANES]
+
+    def take_tile(c):
+        for a in range(2):
+            own[a, c].wait()
+            for p in range(1, n_lon):
+                sends[a, c, p].wait_recv()
+        process(c, lon * own_tiles + c)
+
+    def take_piece():
+        for a in range(2):
+            for p in range(1, n_lon):
+                sends[a, "piece", p].wait_recv()
+        gap = jnp.zeros((LANES - piece, depth), jnp.float32)
+        for a in range(2):
+            pr[a, lon] = ps[a, lon]
+            for q in range(n_lon):
+                rx[a, own_tiles, q] = jnp.concatenate([pr[a, q], gap], axis=0).T[:rows]
+        process(own_tiles, tiles + lon)
+
+    take_tile(0)
+    for c in range(1, own_tiles):
+        take_tile(c) if c == 1 else None
+    take_piece()
+    for c in range(2, own_tiles):
+        take_tile(c)
+
+    size = acc.shape[0]
+    s_half, s_quart = size // 2, size // (2 * n_lon)
+    s_piece = s_quart // n_z
+
+    def exchange(index, src, dst, device):
+        copy = pltpu.make_async_remote_copy(
+            src_ref=src, dst_ref=dst, send_sem=ss.at[index], recv_sem=sr.at[index],
+            device_id=device, device_id_type=MESH,
+        )
+        copy.start()
+        return copy
+
+    def part(start, length):
+        return pl.ds(pl.multiple_of(start, 8), length)
+
+    def settle(copies):
+        for c in copies:
+            c.wait()
+
+    settle([exchange(0, acc.at[part((1 - core) * s_half, s_half)], r0, sibling)])
+    half[...] = acc[part(core * s_half, s_half), :] + r0[...]
+    settle([
+        exchange(p, half.at[part((lon + p) % n_lon * s_quart, s_quart)], r1.at[p - 1], lon_peer(p))
+        for p in range(1, n_lon)
+    ])
+    quart[...] = half[part(lon * s_quart, s_quart), :] + r1[0] + r1[1] + r1[2]
+    base = n_lon
+    settle([
+        exchange(base + p - 1, quart.at[part((z + p) % n_z * s_piece, s_piece)], r2.at[p - 1], z_peer(p))
+        for p in range(1, n_z)
+    ])
+    done = quart[part(z * s_piece, s_piece), :]
+    for p in range(1, n_z):
+        done = done + r2[p - 1]
+    mine = part(core * s_half + lon * s_quart + z * s_piece, s_piece)
+    full[mine, :] = done
+    base += n_z - 1
+    settle([exchange(base + p - 1, full.at[mine], full.at[mine], z_peer(p)) for p in range(1, n_z)])
+    base += n_z - 1
+    mine = part(core * s_half + lon * s_quart, s_quart)
+    settle([exchange(base + p - 1, full.at[mine], full.at[mine], lon_peer(p)) for p in range(1, n_lon)])
+    base += n_lon - 1
+    mine = part(core * s_half, s_half)
+    settle([exchange(base, full.at[mine], full.at[mine], sibling)])
+    for c in sends.values():
+        c.wait_send()
+
+    for t in range(-(-waves // LANES)):
+        width = min(LANES, waves - t * LANES)
+        for curve in range(3):
+            at = t * n_rows + curve * FIELDS
+            energy[curve, :, t * LANES : t * LANES + width] = full[at : at + FIELDS, :width]
+    means = full[n_rows - 4 : n_rows, :]
+    m_ee, m_ft, m_ff, m_tt = means[0:1], means[1:2], means[2:3], means[3:4]
+    skill[0:1, :] = jnp.sqrt(m_ee)
+    skill[1:2, :] = m_ft / jnp.sqrt((m_ff + epsilon) * (m_tt + epsilon))
+
+
+def fused(lat_devices, lon_devices, predicted_state, verified_state, normal_state):
+    rows, cols = predicted_state.shape
+    total = rows * lon_devices
+    waves = total // 2 + 1
+    tab_hi, tab_lo, field, weight = plan_constants(rows, cols, lat_devices, lon_devices)
+    depth = tab_hi.shape[2]
+    per_class = tab_hi.shape[1] // 2
+    tiles = cols // LANES
+    own_tiles = tiles // lon_devices
+    piece = LANES // lon_devices
+    spread = -(-4 * per_class // LANES) * LANES
+    n_rows = 3 * FIELDS + 4
+    n_z = lat_devices // 2
+    unit = 8 * lat_devices * lon_devices
+    size = -(-(spread // LANES) * n_rows // unit) * unit
+    f32, b16 = jnp.float32, jnp.bfloat16
+    copies = 2 * (lon_devices + n_z - 1)
+    dma = pltpu.SemaphoreType.DMA
+    scratch = [
+        pltpu.VMEM((rows, cols), f32), pltpu.VMEM((rows, cols), f32), pltpu.VMEM((rows, cols), f32),
+        pltpu.VMEM((2, own_tiles + 1, lon_devices, rows, LANES), f32),
+        pltpu.VMEM((2, lon_devices, piece, depth), f32),
+        pltpu.VMEM((2, lon_devices, piece, depth), f32),
+        pltpu.VMEM((depth, 8 * LANES), b16), pltpu.VMEM((depth, 8 * LANES), b16),
+        pltpu.VMEM((3, spread, LANES), f32),
+        pltpu.VMEM((size, LANES), f32),
+        pltpu.VMEM((size // 2, LANES), f32), pltpu.VMEM((size // 2, LANES), f32),
+        pltpu.VMEM((lon_devices - 1, size // (2 * lon_devices), LANES), f32),
+        pltpu.VMEM((size // (2 * lon_devices), LANES), f32),
+        pltpu.VMEM((n_z - 1, size // (2 * lon_devices * n_z), LANES), f32),
+        pltpu.VMEM((size, LANES), f32),
+        dma((3,)), dma((2, own_tiles)),
+        dma((2, own_tiles, lon_devices - 1)), dma((2, own_tiles, lon_devices - 1)),
+        dma((2, lon_devices - 1)), dma((2, lon_devices - 1)),
+        dma((copies,)), dma((copies,)),
+    ]
+    any_spec = pl.BlockSpec(memory_space=pl.ANY)
+    vmem = pl.BlockSpec(memory_space=pltpu.VMEM)
+    dims = (rows, cols, lat_devices, lon_devices, total)
+    energy, skill = pl.pallas_call(
+        functools.partial(kernel, dims),
+        out_shape=(
+            jax.ShapeDtypeStruct((3, FIELDS, waves), f32),
+            jax.ShapeDtypeStruct((2, LANES), f32),
+        ),
+        in_specs=[any_spec] * 3 + [vmem] * 4,
+        out_specs=(vmem, vmem),
+        scratch_shapes=scratch,
+        compiler_params=pltpu.CompilerParams(
+            collective_id=0, has_side_effects=True, vmem_limit_bytes=60_000_000
+        ),
+    )(predicted_state, verified_state, normal_state, jnp.asarray(tab_hi), jnp.asarray(tab_lo), jnp.asarray(field), jnp.asarray(weight))
+    return energy, skill[0, :FIELDS], skill[1, :FIELDS]
+
+
 def solution(mesh):
     in_specs = (P("lon", "lat"), P("lon", "lat"), P("lon", "lat"))
     out_specs = (P(), P(), P())
-    return jax.shard_map(local, mesh=mesh, in_specs=in_specs, out_specs=out_specs, check_vma=False)
+    n_lat, n_lon = mesh.shape["lat"], mesh.shape["lon"]
+
+    def body(predicted_state, verified_state, normal_state):
+        rows, cols = predicted_state.shape
+        fits = (
+            n_lon == 4 and n_lat % 2 == 0 and n_lat > 2 and rows % 8 == 0
+            and cols % LANES == 0 and cols // LANES % n_lon == 1 and cols // LANES // n_lon >= 2
+        )
+        if fits:
+            return fused(n_lat, n_lon, predicted_state, verified_state, normal_state)
+        return local(predicted_state, verified_state, normal_state)
+
+    return jax.shard_map(body, mesh=mesh, in_specs=in_specs, out_specs=out_specs, check_vma=False)

time: 276 us -> 89.4 us (0.32)
  Pallas kernels: 0 us -> 85.4 us
  waiting for transfers between devices: 75.7 us -> 0 us
  blocking collectives: 67.7 us -> 0 us
  local copies, waits for them, and re-layouts: 42.8 us -> 3.12 us
  matrix products: 35 us -> 0 us
  other arithmetic: 29 us -> 0 us
  between operations: 15.5 us -> 0.64 us
  starting transfers between devices: 9.01 us -> 0 us
    pallas_call x0 -> x1, Pallas kernels: none -> 85.4 us  [fused(): pl.pallas_call(functools.partial(kernel, dims), out_shape=(jax.ShapeDtype...]
    psum x1 -> x0, blocking collectives: 57.3 us -> none  [local(): lax.psum(skill_terms, ('lat', 'lon')) / (lon_total * weight_total)]
    psum x1 -> x0, waiting for transfers between devices: 51.8 us -> none  [local(): band_sum = lax.psum(band_sum, 'lat')]
    dot_general x3 -> x0, matrix products: 35 us -> none  [the longest x1 29.4 us: transform_columns(): lax.dot_general(stacked, table, (((0,), (0,)), ((), ())), precision=lax.P...]
    all_to_all x2 -> x0, waiting for transfers between devices: 23.8 us -> none  [the longest x1 23.8 us: local(): lax.all_to_all(true_blocks, 'lon', split_axis=1, concat_axis=0, tiled=True)]
    neg x1 -> x0, other arithmetic: 19.7 us -> none  [dft_table(): return jnp.concatenate([jnp.cos(angle), -jnp.sin(angle)], axis=1)]
    all_gather x1 -> x0, blocking collectives: 10.4 us -> none  [local(): gathered = lax.all_gather(band_sum, 'lon', axis=0, tiled=True)]
    reshape x4 -> x0, local copies, waits for them, and re-layouts: 10.2 us -> none  [the longest x1 4.86 us: local(): weighted = powers.reshape(row_share, 3 * wave_count) * row_scale[:, None]]
  transfers between devices with their start and end apart: 3 -> 0, of which waited for: 2 -> 0; matrix products, arithmetic and copies ran while one was open for 15% -> 0% of each run, Pallas kernels for 0% -> 0%
where the time goes in v1:
time: 89.4 us; the launch traced here: 89.2 us
  Pallas kernels  85.4 us (96%)
  local copies, waits for them, and re-layouts  3.12 us (3%)
    pallas_call x1, Pallas kernels, fused(): pl.pallas_call(functools.partial(kernel, dims), out_shape=(jax.ShapeDtype...  85.4 us
    unnamed x1, local copies, waits for them, and re-layouts  1.86 us

profile of v1, /device:TPU:0, one launch (start us, length us, event | category | flops | bytes accessed | tf_op | source)
XLA Modules:
  0.0 89.2 jit_solution(14639683573841774631)
XLA Ops:
  0.6 85.4 %shard_map.94 = (f32[3,52,721]{2,1,0:T(8,128)}, f32[2,128]{1,0:T(2,128)}) custom-call(f32[360,1664]{1,0:T(8,128)} %fore.1, f32[360,1664]{1,0:T(8,128)} %true.1, f32[360,1664]{1,0:T(8,128)} %norm.1, bf16[4,368,384]{2,1,0:T(8,128)(2,1)} %constant.8.clone.tab_hi, bf16[4,368,384]{2,1,0:T(8,128)(2,1)} %constant.9.clone.tab_lo, s32[17,128]{1,0:T(8,128)} %constant.10.clone.field, ...), custom_call_target="tpu_custom_call" | custom-call | tf_op jit(solution)/shard_map/pallas_call | solution.py:467
  86.1 1.3 %slice_bitcast_fusion = (f32[52]{0:T(128)}, f32[52]{0:T(128)}) fusion(f32[2,128]{1,0:T(2,128)} %get-tuple-element.6), kind=kLoop, calls=%fused_computation | loop fusion | bytes 832 | tf_op jit(solution)/shard_map/squeeze | solution.py:480
  87.3 1.9 %copy.11 = f32[3,52,721]{2,1,0:T(8,128)} copy(f32[3,52,721]{2,1,0:T(8,128)} %get-tuple-element.12) | data formatting | bytes 899808

commit v2 on v1

--- a/solution.py
+++ b/solution.py
@@ -11,6 +11,7 @@
 FIELDS = 52
 LANES = 128
 MESH = pl.DeviceIdType.MESH
+ORDER = (3, 1, 2)
 
 
 epsilon = 1e-06
@@ -166,10 +167,10 @@
 
 
 def kernel(
-    dims, fore, true, norm, tab_hi, tab_lo, field, weight,
-    energy, skill,
+    dims, fore, true, norm, hi_hbm, lo_hbm, field, weight,
+    result,
     fb, tb, nb, rx, ps, pr, bhi, blo, pbuf, acc, r0, half, r1, quart, r2, full,
-    load_sem, own_sem, xs, xr, qs, qr, ss, sr,
+    load_sem, own_sem, xs, xr, qs, qr, ss, sr, tab_hi, tab_lo,
 ):
     rows, cols, n_lat, n_lon, total = dims
     n_z = n_lat // 2
@@ -187,8 +188,10 @@
     n_rows = 3 * FIELDS + 4
     sibling = {"lat": lat + 1 - 2 * core, "lon": lon}
 
+    flips = (lon, lon + 1 - 2 * (lon % 2), lon + 2 - 4 * (lon // 2), n_lon - 1 - lon)
+
     def lon_peer(p):
-        return {"lat": lat, "lon": (lon + p) % n_lon}
+        return {"lat": lat, "lon": flips[p]}
 
     def z_peer(p):
         return {"lat": (z + p) % n_z * 2 + core, "lon": lon}
@@ -199,7 +202,7 @@
         pl.semaphore_signal(barrier, inc=1, device_id=d, device_id_type=MESH)
     loads = [
         pltpu.make_async_copy(src, dst, load_sem.at[i])
-        for i, (src, dst) in enumerate(((fore, fb), (true, tb), (norm, nb)))
+        for i, (src, dst) in enumerate(((fore, fb), (true, tb), (norm, nb), (hi_hbm, tab_hi), (lo_hbm, tab_lo)))
     ]
     for c in loads:
         c.start()
@@ -220,9 +223,9 @@
     sends = {}
 
     def send_tile(c):
-        for p in (2, 1, 3) if n_lon == 4 else range(1, n_lon):
+        for p in ORDER:
             for a in range(2):
-                dest = (lon + p) % n_lon
+                dest = flips[p]
                 sends[a, c, p] = pltpu.make_async_remote_copy(
                     src_ref=tile_ref(a, dest * own_tiles + c),
                     dst_ref=rx.at[a, c, lon],
@@ -243,10 +246,10 @@
         ps[a] = flipped.reshape(n_lon, piece, depth)
     for c in range(1, own_tiles):
         send_tile(c) if c == 1 else None
-    for p in range(1, n_lon):
+    for p in ORDER:
         for a in range(2):
             sends[a, "piece", p] = pltpu.make_async_remote_copy(
-                src_ref=ps.at[a, (lon + p) % n_lon],
+                src_ref=ps.at[a, flips[p]],
                 dst_ref=pr.at[a, lon],
                 send_sem=qs.at[a, p - 1],
                 recv_sem=qr.at[a, p - 1],
@@ -360,6 +363,8 @@
                 rx[a, own_tiles, q] = jnp.concatenate([pr[a, q], gap], axis=0).T[:rows]
         process(own_tiles, tiles + lon)
 
+    loads[3].wait()
+    loads[4].wait()
     take_tile(0)
     for c in range(1, own_tiles):
         take_tile(c) if c == 1 else None
@@ -382,38 +387,82 @@
     def part(start, length):
         return pl.ds(pl.multiple_of(start, 8), length)
 
-    def settle(copies):
-        for c in copies:
-            c.wait()
-
-    settle([exchange(0, acc.at[part((1 - core) * s_half, s_half)], r0, sibling)])
-    half[...] = acc[part(core * s_half, s_half), :] + r0[...]
-    settle([
-        exchange(p, half.at[part((lon + p) % n_lon * s_quart, s_quart)], r1.at[p - 1], lon_peer(p))
-        for p in range(1, n_lon)
-    ])
-    quart[...] = half[part(lon * s_quart, s_quart), :] + r1[0] + r1[1] + r1[2]
+    def quarter(j):
+        return flips[j] * s_quart
+
+    near_first, far_first = (1, 2, 3), (3, 1, 2)
+    z_order = (2, 1, 3, 0)
+    cross = {
+        j: exchange(
+            j, acc.at[part((1 - core) * s_half + quarter(j), s_quart)],
+            r0.at[part(quarter(j), s_quart)], sibling,
+        )
+        for j in (*far_first, 0)
+    }
     base = n_lon
-    settle([
-        exchange(base + p - 1, quart.at[part((z + p) % n_z * s_piece, s_piece)], r2.at[p - 1], z_peer(p))
-        for p in range(1, n_z)
-    ])
+    over_lon = {}
+    for j in (*far_first, 0):
+        cross[j].wait_recv()
+        rows_j = part(quarter(j), s_quart)
+        half[rows_j, :] = acc[part(core * s_half + quarter(j), s_quart), :] + r0[rows_j, :]
+        if j > 0:
+            for p in z_order:
+                at = (z + p) % n_z * s_piece
+                over_lon[j, p] = exchange(
+                    base + (j - 1) * n_z + p, half.at[part(quarter(j) + at, s_piece)],
+                    r1.at[j - 1, part(at, s_piece)], lon_peer(j),
+                )
+    base += (n_lon - 1) * n_z
+    over_z = {}
+    for p in z_order:
+        for j in range(1, n_lon):
+            over_lon[j, p].wait_recv()
+        at = (z + p) % n_z * s_piece
+        rows_p = part(at, s_piece)
+        quart[rows_p, :] = (
+            half[part(quarter(0) + at, s_piece), :] + r1[0, rows_p, :] + r1[1, rows_p, :] + r1[2, rows_p, :]
+        )
+        if p > 0:
+            over_z[p] = exchange(base + p - 1, quart.at[rows_p], r2.at[p - 1], z_peer(p))
+    base += n_z - 1
     done = quart[part(z * s_piece, s_piece), :]
     for p in range(1, n_z):
+        over_z[p].wait_recv()
         done = done + r2[p - 1]
-    mine = part(core * s_half + lon * s_quart + z * s_piece, s_piece)
+    quarter_at = core * s_half + quarter(0)
+    mine = part(quarter_at + z * s_piece, s_piece)
     full[mine, :] = done
+
+    back_z = {p: exchange(base + p - 1, full.at[mine], full.at[mine], z_peer(p)) for p in (2, 1, 3)}
     base += n_z - 1
-    settle([exchange(base + p - 1, full.at[mine], full.at[mine], z_peer(p)) for p in range(1, n_z)])
-    base += n_z - 1
-    mine = part(core * s_half + lon * s_quart, s_quart)
-    settle([exchange(base + p - 1, full.at[mine], full.at[mine], lon_peer(p)) for p in range(1, n_lon)])
-    base += n_lon - 1
-    mine = part(core * s_half, s_half)
-    settle([exchange(base, full.at[mine], full.at[mine], sibling)])
+    back_lon = {}
+    for p in (0, 1, 3, 2):
+        if p > 0:
+            back_z[p].wait_recv()
+        rows_p = part(quarter_at + (z + n_z - p) % n_z * s_piece, s_piece)
+        for j in far_first:
+            back_lon[j, p] = exchange(base + (j - 1) * n_z + p, full.at[rows_p], full.at[rows_p], lon_peer(j))
+    base += (n_lon - 1) * n_z
+    back_core = {}
+    for j in (0, *near_first):
+        if j > 0:
+            for p in range(n_z):
+                back_lon[j, p].wait_recv()
+        rows_j = part(core * s_half + quarter(j), s_quart)
+        back_core[j] = exchange(base + j, full.at[rows_j], full.at[rows_j], sibling)
+    for c in back_core.values():
+        c.wait_recv()
+    for group in (cross, over_lon, over_z, back_z, back_lon, back_core):
+        for c in group.values():
+            c.wait_send()
     for c in sends.values():
         c.wait_send()
 
+    result[...] = full[...]
+
+
+def finish(waves, full, energy, rms, corr):
+    n_rows = 3 * FIELDS + 4
     for t in range(-(-waves // LANES)):
         width = min(LANES, waves - t * LANES)
         for curve in range(3):
@@ -421,8 +470,8 @@
             energy[curve, :, t * LANES : t * LANES + width] = full[at : at + FIELDS, :width]
     means = full[n_rows - 4 : n_rows, :]
     m_ee, m_ft, m_ff, m_tt = means[0:1], means[1:2], means[2:3], means[3:4]
-    skill[0:1, :] = jnp.sqrt(m_ee)
-    skill[1:2, :] = m_ft / jnp.sqrt((m_ff + epsilon) * (m_tt + epsilon))
+    rms[...] = jnp.sqrt(m_ee)[0, :FIELDS]
+    corr[...] = (m_ft / jnp.sqrt((m_ff + epsilon) * (m_tt + epsilon)))[0, :FIELDS]
 
 
 def fused(lat_devices, lon_devices, predicted_state, verified_state, normal_state):
@@ -441,7 +490,7 @@
     unit = 8 * lat_devices * lon_devices
     size = -(-(spread // LANES) * n_rows // unit) * unit
     f32, b16 = jnp.float32, jnp.bfloat16
-    copies = 2 * (lon_devices + n_z - 1)
+    copies = 2 * (lon_devices + lon_devices * n_z)
     dma = pltpu.SemaphoreType.DMA
     scratch = [
         pltpu.VMEM((rows, cols), f32), pltpu.VMEM((rows, cols), f32), pltpu.VMEM((rows, cols), f32),
@@ -456,28 +505,35 @@
         pltpu.VMEM((size // (2 * lon_devices), LANES), f32),
         pltpu.VMEM((n_z - 1, size // (2 * lon_devices * n_z), LANES), f32),
         pltpu.VMEM((size, LANES), f32),
-        dma((3,)), dma((2, own_tiles)),
+        dma((5,)), dma((2, own_tiles)),
         dma((2, own_tiles, lon_devices - 1)), dma((2, own_tiles, lon_devices - 1)),
         dma((2, lon_devices - 1)), dma((2, lon_devices - 1)),
         dma((copies,)), dma((copies,)),
+        pltpu.VMEM(tab_hi.shape, b16), pltpu.VMEM(tab_lo.shape, b16),
     ]
     any_spec = pl.BlockSpec(memory_space=pl.ANY)
     vmem = pl.BlockSpec(memory_space=pltpu.VMEM)
     dims = (rows, cols, lat_devices, lon_devices, total)
-    energy, skill = pl.pallas_call(
+    summed = pl.pallas_call(
         functools.partial(kernel, dims),
-        out_shape=(
-            jax.ShapeDtypeStruct((3, FIELDS, waves), f32),
-            jax.ShapeDtypeStruct((2, LANES), f32),
-        ),
-        in_specs=[any_spec] * 3 + [vmem] * 4,
-        out_specs=(vmem, vmem),
+        out_shape=jax.ShapeDtypeStruct((size, LANES), f32),
+        in_specs=[any_spec] * 5 + [vmem] * 2,
+        out_specs=vmem,
         scratch_shapes=scratch,
         compiler_params=pltpu.CompilerParams(
             collective_id=0, has_side_effects=True, vmem_limit_bytes=60_000_000
         ),
     )(predicted_state, verified_state, normal_state, jnp.asarray(tab_hi), jnp.asarray(tab_lo), jnp.asarray(field), jnp.asarray(weight))
-    return energy, skill[0, :FIELDS], skill[1, :FIELDS]
+    return pl.pallas_call(
+        functools.partial(finish, waves),
+        out_shape=(
+            jax.ShapeDtypeStruct((3, FIELDS, waves), f32),
+            jax.ShapeDtypeStruct((FIELDS,), f32),
+            jax.ShapeDtypeStruct((FIELDS,), f32),
+        ),
+        in_specs=[vmem],
+        out_specs=(vmem, vmem, vmem),
+    )(summed)
 
 
 def solution(mesh):

time: 89.4 us -> 85.9 us (0.961)
  local copies, waits for them, and re-layouts: 3.12 us -> 0 us
    unnamed x1 -> x0, local copies, waits for them, and re-layouts: 1.86 us -> none
    squeeze x1 -> x0, local copies, waits for them, and re-layouts: 1.26 us -> none  [fused(): return (energy, skill[0, :FIELDS], skill[1, :FIELDS])]
    pallas_call x1 -> x2, Pallas kernels: 85.4 us -> 85.1 us  [the longest x1 83.2 us: fused(): pl.pallas_call(functools.partial(kernel, dims), out_shape=jax.ShapeDtypeS...]
where the time goes in v2:
time: 85.9 us; the launch traced here: 85.7 us
  Pallas kernels  85.1 us (99%)
    pallas_call x1, Pallas kernels, fused(): pl.pallas_call(functools.partial(kernel, dims), out_shape=jax.ShapeDtypeS...  83.2 us
    pallas_call x1, Pallas kernels, fused(): pl.pallas_call(functools.partial(finish, waves), out_shape=(jax.ShapeDtyp...  1.87 us

profile of v2, /device:TPU:0, one launch (start us, length us, event | category | flops | bytes accessed | tf_op | source)
XLA Modules:
  0.0 85.7 jit_solution(15344697111010440287)
XLA Ops:
  0.6 83.2 %shard_map.94.full = f32[1024,128]{1,0:T(8,128)} custom-call(f32[360,1664]{1,0:T(8,128)} %fore.1, f32[360,1664]{1,0:T(8,128)} %true.1, f32[360,1664]{1,0:T(8,128)} %norm.1, bf16[4,368,384]{2,1,0:T(8,128)(2,1)} %constant.8.clone.hi_hbm, bf16[4,368,384]{2,1,0:T(8,128)(2,1)} %constant.9.clone.lo_hbm, s32[17,128]{1,0:T(8,128)} %constant.10.clone.field, ...), custom_call_target="tpu_custom_call" | custom-call | tf_op jit(solution)/shard_map/pallas_call | solution.py:517
  83.8 1.9 %shard_map.95 = (f32[3,52,721]{2,1,0:T(8,128)}, f32[52]{0:T(128)}, f32[52]{0:T(128)}) custom-call(f32[1024,128]{1,0:T(8,128)} %shard_map.94.full), custom_call_target="tpu_custom_call" | custom-call | tf_op jit(solution)/shard_map/pallas_call | solution.py:527

commit v3 on v2

--- a/solution.py
+++ b/solution.py
@@ -167,10 +167,10 @@
 
 
 def kernel(
-    dims, fore, true, norm, hi_hbm, lo_hbm, field, weight,
+    dims, fore, true, norm, hi_hbm, lo_hbm, field_hbm, weight_hbm,
     result,
-    fb, tb, nb, rx, ps, pr, bhi, blo, pbuf, acc, r0, half, r1, quart, r2, full,
-    load_sem, own_sem, xs, xr, qs, qr, ss, sr, tab_hi, tab_lo,
+    fb, tb, nb, rx, ps, pr, stack, pbuf, acc, r0, half, r1, quart, r2, full,
+    load_sem, own_sem, xs, xr, qs, qr, ss, sr, tab, field, weight,
 ):
     rows, cols, n_lat, n_lon, total = dims
     n_z = n_lat // 2
@@ -182,8 +182,8 @@
     own_tiles = tiles // n_lon
     slots = tiles + n_lon
     piece = LANES // n_lon
-    depth = tab_hi.shape[2]
-    per_class = tab_hi.shape[1] // 2
+    depth = tab.shape[2] // 3
+    per_class = tab.shape[1] // 2
     waves = total // 2 + 1
     n_rows = 3 * FIELDS + 4
     sibling = {"lat": lat + 1 - 2 * core, "lon": lon}
@@ -200,24 +200,11 @@
     peers = [sibling] + [lon_peer(p) for p in range(1, n_lon)] + [z_peer(p) for p in range(1, n_z)]
     for d in peers:
         pl.semaphore_signal(barrier, inc=1, device_id=d, device_id_type=MESH)
-    loads = [
-        pltpu.make_async_copy(src, dst, load_sem.at[i])
-        for i, (src, dst) in enumerate(((fore, fb), (true, tb), (norm, nb), (hi_hbm, tab_hi), (lo_hbm, tab_lo)))
-    ]
-    for c in loads:
-        c.start()
     sources = (fore, true)
 
     def tile_ref(a, t):
         return sources[a].at[:, pl.ds(pl.multiple_of(t * LANES, LANES), LANES)]
 
-    own = {}
-    for c in range(own_tiles):
-        for a in range(2):
-            own[a, c] = pltpu.make_async_copy(
-                tile_ref(a, lon * own_tiles + c), rx.at[a, c, lon], own_sem.at[a, c]
-            )
-            own[a, c].start()
     pl.semaphore_wait(barrier, len(peers))
 
     sends = {}
@@ -237,6 +224,23 @@
                 sends[a, c, p].start()
 
     send_tile(0)
+    send_tile(1)
+    loads = [
+        pltpu.make_async_copy(src, dst, load_sem.at[i])
+        for i, (src, dst) in enumerate((
+            (fore, fb), (true, tb), (norm, nb), (field_hbm, field), (weight_hbm, weight),
+            (hi_hbm, tab.at[:, :, :depth]), (hi_hbm, tab.at[:, :, depth : 2 * depth]), (lo_hbm, tab.at[:, :, 2 * depth :]),
+        ))
+    ]
+    for c in loads:
+        c.start()
+    own = {}
+    for c in range(own_tiles):
+        for a in range(2):
+            own[a, c] = pltpu.make_async_copy(
+                tile_ref(a, lon * own_tiles + c), rx.at[a, c, lon], own_sem.at[a, c]
+            )
+            own[a, c].start()
     loads[0].wait()
     loads[1].wait()
     last = (tiles - 1) * LANES
@@ -244,8 +248,6 @@
     for a, block in enumerate((fb, tb)):
         flipped = jnp.concatenate([block[:, last : last + LANES], pad], axis=0).T
         ps[a] = flipped.reshape(n_lon, piece, depth)
-    for c in range(1, own_tiles):
-        send_tile(c) if c == 1 else None
     for p in ORDER:
         for a in range(2):
             sends[a, "piece", p] = pltpu.make_async_remote_copy(
@@ -262,7 +264,8 @@
 
     acc[...] = jnp.zeros_like(acc)
     pbuf[...] = jnp.zeros_like(pbuf)
-    loads[2].wait()
+    for c in loads[2:5]:
+        c.wait()
     field_rows = lax.broadcasted_iota(jnp.int32, (LANES, LANES), 0)
 
     def skill_tile(t, carry):
@@ -294,17 +297,12 @@
         hi = y.astype(jnp.bfloat16)
         lo = (y - hi.astype(jnp.float32)).astype(jnp.bfloat16)
         at = group * 2 * LANES + a * LANES
-        bhi[:, at : at + LANES] = hi
-        blo[:, at : at + LANES] = lo
+        stack[:depth, at : at + LANES] = hi
+        stack[depth : 2 * depth, at : at + LANES] = lo
+        stack[2 * depth :, at : at + LANES] = hi
 
     def product(r, start, width):
-        cut = slice(start, start + width)
-        th, tl = tab_hi[r], tab_lo[r]
-        return (
-            jnp.dot(th, bhi[:, cut], preferred_element_type=jnp.float32)
-            + jnp.dot(th, blo[:, cut], preferred_element_type=jnp.float32)
-            + jnp.dot(tl, bhi[:, cut], preferred_element_type=jnp.float32)
-        )
+        return jnp.dot(tab[r], stack[:, start : start + width], preferred_element_type=jnp.float32)
 
     def process(c, slot):
         for a in range(2):
@@ -363,11 +361,10 @@
                 rx[a, own_tiles, q] = jnp.concatenate([pr[a, q], gap], axis=0).T[:rows]
         process(own_tiles, tiles + lon)
 
-    loads[3].wait()
-    loads[4].wait()
+    for c in loads[5:]:
+        c.wait()
     take_tile(0)
-    for c in range(1, own_tiles):
-        take_tile(c) if c == 1 else None
+    take_tile(1)
     take_piece()
     for c in range(2, own_tiles):
         take_tile(c)
@@ -497,7 +494,7 @@
         pltpu.VMEM((2, own_tiles + 1, lon_devices, rows, LANES), f32),
         pltpu.VMEM((2, lon_devices, piece, depth), f32),
         pltpu.VMEM((2, lon_devices, piece, depth), f32),
-        pltpu.VMEM((depth, 8 * LANES), b16), pltpu.VMEM((depth, 8 * LANES), b16),
+        pltpu.VMEM((3 * depth, 8 * LANES), b16),
         pltpu.VMEM((3, spread, LANES), f32),
         pltpu.VMEM((size, LANES), f32),
         pltpu.VMEM((size // 2, LANES), f32), pltpu.VMEM((size // 2, LANES), f32),
@@ -505,11 +502,12 @@
         pltpu.VMEM((size // (2 * lon_devices), LANES), f32),
         pltpu.VMEM((n_z - 1, size // (2 * lon_devices * n_z), LANES), f32),
         pltpu.VMEM((size, LANES), f32),
-        dma((5,)), dma((2, own_tiles)),
+        dma((8,)), dma((2, own_tiles)),
         dma((2, own_tiles, lon_devices - 1)), dma((2, own_tiles, lon_devices - 1)),
         dma((2, lon_devices - 1)), dma((2, lon_devices - 1)),
         dma((copies,)), dma((copies,)),
-        pltpu.VMEM(tab_hi.shape, b16), pltpu.VMEM(tab_lo.shape, b16),
+        pltpu.VMEM((4, 2 * per_class, 3 * depth), b16),
+        pltpu.VMEM(field.shape, jnp.int32), pltpu.VMEM(weight.shape, f32),
     ]
     any_spec = pl.BlockSpec(memory_space=pl.ANY)
     vmem = pl.BlockSpec(memory_space=pltpu.VMEM)
@@ -517,7 +515,7 @@
     summed = pl.pallas_call(
         functools.partial(kernel, dims),
         out_shape=jax.ShapeDtypeStruct((size, LANES), f32),
-        in_specs=[any_spec] * 5 + [vmem] * 2,
+        in_specs=[any_spec] * 7,
         out_specs=vmem,
         scratch_shapes=scratch,
         compiler_params=pltpu.CompilerParams(

time: 85.9 us -> 84.7 us (0.986)
  Pallas kernels: 85.1 us -> 83.9 us
    pallas_call x1, Pallas kernels: 83.2 us -> 82 us  [fused(): pl.pallas_call(functools.partial(kernel, dims), out_shape=jax.ShapeDtypeS...]
where the time goes in v3:
time: 84.7 us; the launch traced here: 84.6 us
  Pallas kernels  83.9 us (99%)
    pallas_call x1, Pallas kernels, fused(): pl.pallas_call(functools.partial(kernel, dims), out_shape=jax.ShapeDtypeS...  82 us
    pallas_call x1, Pallas kernels, fused(): pl.pallas_call(functools.partial(finish, waves), out_shape=(jax.ShapeDtyp...  1.87 us

profile of v3, /device:TPU:0, one launch (start us, length us, event | category | flops | bytes accessed | tf_op | source)
XLA Modules:
  0.0 84.6 jit_solution(3663246869468891513)
XLA Ops:
  0.6 82.0 %shard_map.94.full = f32[1024,128]{1,0:T(8,128)} custom-call(f32[360,1664]{1,0:T(8,128)} %fore.1, f32[360,1664]{1,0:T(8,128)} %true.1, f32[360,1664]{1,0:T(8,128)} %norm.1, bf16[4,368,384]{2,1,0:T(8,128)(2,1)} %constant.8.clone.hi_hbm, bf16[4,368,384]{2,1,0:T(8,128)(2,1)} %constant.9.clone.lo_hbm, s32[17,128]{1,0:T(8,128)} %constant.10.clone.field_hbm, ...), custom_call_target="tpu_custom_call" | custom-call | tf_op jit(solution)/shard_map/pallas_call | solution.py:515
  82.7 1.9 %shard_map.95 = (f32[3,52,721]{2,1,0:T(8,128)}, f32[52]{0:T(128)}, f32[52]{0:T(128)}) custom-call(f32[1024,128]{1,0:T(8,128)} %shard_map.94.full), custom_call_target="tpu_custom_call" | custom-call | tf_op jit(solution)/shard_map/pallas_call | solution.py:525

commit v4 on v3

--- a/solution.py
+++ b/solution.py
@@ -169,7 +169,7 @@
 def kernel(
     dims, fore, true, norm, hi_hbm, lo_hbm, field_hbm, weight_hbm,
     result,
-    fb, tb, nb, rx, ps, pr, stack, pbuf, acc, r0, half, r1, quart, r2, full,
+    fb, tb, nb, rx, ps, pr, stack, pbuf, acc, r0, half, r1, r2, full,
     load_sem, own_sem, xs, xr, qs, qr, ss, sr, tab, field, weight,
 ):
     rows, cols, n_lat, n_lon, total = dims
@@ -388,7 +388,6 @@
         return flips[j] * s_quart
 
     near_first, far_first = (1, 2, 3), (3, 1, 2)
-    z_order = (2, 1, 3, 0)
     cross = {
         j: exchange(
             j, acc.at[part((1 - core) * s_half + quarter(j), s_quart)],
@@ -403,42 +402,35 @@
         rows_j = part(quarter(j), s_quart)
         half[rows_j, :] = acc[part(core * s_half + quarter(j), s_quart), :] + r0[rows_j, :]
         if j > 0:
-            for p in z_order:
-                at = (z + p) % n_z * s_piece
+            for p in range(n_z):
+                at = p * s_piece
                 over_lon[j, p] = exchange(
                     base + (j - 1) * n_z + p, half.at[part(quarter(j) + at, s_piece)],
                     r1.at[j - 1, part(at, s_piece)], lon_peer(j),
                 )
     base += (n_lon - 1) * n_z
     over_z = {}
-    for p in z_order:
+    z_order = (2, 1, 3)
+    for s in range(n_z):
         for j in range(1, n_lon):
-            over_lon[j, p].wait_recv()
-        at = (z + p) % n_z * s_piece
-        rows_p = part(at, s_piece)
-        quart[rows_p, :] = (
-            half[part(quarter(0) + at, s_piece), :] + r1[0, rows_p, :] + r1[1, rows_p, :] + r1[2, rows_p, :]
-        )
-        if p > 0:
-            over_z[p] = exchange(base + p - 1, quart.at[rows_p], r2.at[p - 1], z_peer(p))
-    base += n_z - 1
-    done = quart[part(z * s_piece, s_piece), :]
-    for p in range(1, n_z):
-        over_z[p].wait_recv()
-        done = done + r2[p - 1]
+            over_lon[j, s].wait_recv()
+        rows_s = pl.ds(s * s_piece, s_piece)
+        r2[z, rows_s, :] = (
+            half[part(quarter(0) + s * s_piece, s_piece), :] + r1[0, rows_s, :] + r1[1, rows_s, :] + r1[2, rows_s, :]
+        )
+        for p in z_order:
+            over_z[p, s] = exchange(base + (p - 1) * n_z + s, r2.at[z, rows_s], r2.at[z, rows_s], z_peer(p))
+    base += (n_z - 1) * n_z
     quarter_at = core * s_half + quarter(0)
-    mine = part(quarter_at + z * s_piece, s_piece)
-    full[mine, :] = done
-
-    back_z = {p: exchange(base + p - 1, full.at[mine], full.at[mine], z_peer(p)) for p in (2, 1, 3)}
-    base += n_z - 1
     back_lon = {}
-    for p in (0, 1, 3, 2):
-        if p > 0:
-            back_z[p].wait_recv()
-        rows_p = part(quarter_at + (z + n_z - p) % n_z * s_piece, s_piece)
+    for s in range(n_z):
+        for p in z_order:
+            over_z[p, s].wait_recv()
+        rows_s = pl.ds(s * s_piece, s_piece)
+        mine = part(quarter_at + s * s_piece, s_piece)
+        full[mine, :] = r2[0, rows_s, :] + r2[1, rows_s, :] + r2[2, rows_s, :] + r2[3, rows_s, :]
         for j in far_first:
-            back_lon[j, p] = exchange(base + (j - 1) * n_z + p, full.at[rows_p], full.at[rows_p], lon_peer(j))
+            back_lon[j, s] = exchange(base + (j - 1) * n_z + s, full.at[mine], full.at[mine], lon_peer(j))
     base += (n_lon - 1) * n_z
     back_core = {}
     for j in (0, *near_first):
@@ -449,7 +441,7 @@
         back_core[j] = exchange(base + j, full.at[rows_j], full.at[rows_j], sibling)
     for c in back_core.values():
         c.wait_recv()
-    for group in (cross, over_lon, over_z, back_z, back_lon, back_core):
+    for group in (cross, over_lon, over_z, back_lon, back_core):
         for c in group.values():
             c.wait_send()
     for c in sends.values():
@@ -487,7 +479,7 @@
     unit = 8 * lat_devices * lon_devices
     size = -(-(spread // LANES) * n_rows // unit) * unit
     f32, b16 = jnp.float32, jnp.bfloat16
-    copies = 2 * (lon_devices + lon_devices * n_z)
+    copies = 3 * lon_devices * n_z
     dma = pltpu.SemaphoreType.DMA
     scratch = [
         pltpu.VMEM((rows, cols), f32), pltpu.VMEM((rows, cols), f32), pltpu.VMEM((rows, cols), f32),
@@ -499,8 +491,7 @@
         pltpu.VMEM((size, LANES), f32),
         pltpu.VMEM((size // 2, LANES), f32), pltpu.VMEM((size // 2, LANES), f32),
         pltpu.VMEM((lon_devices - 1, size // (2 * lon_devices), LANES), f32),
-        pltpu.VMEM((size // (2 * lon_devices), LANES), f32),
-        pltpu.VMEM((n_z - 1, size // (2 * lon_devices * n_z), LANES), f32),
+        pltpu.VMEM((n_z, size // (2 * lon_devices), LANES), f32),
         pltpu.VMEM((size, LANES), f32),
         dma((8,)), dma((2, own_tiles)),
         dma((2, own_tiles, lon_devices - 1)), dma((2, own_tiles, lon_devices - 1)),
@@ -542,7 +533,7 @@
     def body(predicted_state, verified_state, normal_state):
         rows, cols = predicted_state.shape
         fits = (
-            n_lon == 4 and n_lat % 2 == 0 and n_lat > 2 and rows % 8 == 0
+            n_lon == 4 and n_lat == 8 and rows % 8 == 0
             and cols % LANES == 0 and cols // LANES % n_lon == 1 and cols // LANES // n_lon >= 2
         )
         if fits:

time: 84.7 us -> 83.4 us (0.985)
  Pallas kernels: 83.9 us -> 82.6 us
    pallas_call x1, Pallas kernels: 82 us -> 80.7 us  [fused(): pl.pallas_call(functools.partial(kernel, dims), out_shape=jax.ShapeDtypeS...]
where the time goes in v4:
time: 83.4 us; the launch traced here: 83.3 us
  Pallas kernels  82.6 us (99%)
    pallas_call x1, Pallas kernels, fused(): pl.pallas_call(functools.partial(kernel, dims), out_shape=jax.ShapeDtypeS...  80.7 us
    pallas_call x1, Pallas kernels, fused(): pl.pallas_call(functools.partial(finish, waves), out_shape=(jax.ShapeDtyp...  1.87 us

profile of v4, /device:TPU:0, one launch (start us, length us, event | category | flops | bytes accessed | tf_op | source)
XLA Modules:
  0.0 83.3 jit_solution(1471389865957124189)
XLA Ops:
  0.6 80.7 %shard_map.94.full = f32[1024,128]{1,0:T(8,128)} custom-call(f32[360,1664]{1,0:T(8,128)} %fore.1, f32[360,1664]{1,0:T(8,128)} %true.1, f32[360,1664]{1,0:T(8,128)} %norm.1, bf16[4,368,384]{2,1,0:T(8,128)(2,1)} %constant.8.clone.hi_hbm, bf16[4,368,384]{2,1,0:T(8,128)(2,1)} %constant.9.clone.lo_hbm, s32[17,128]{1,0:T(8,128)} %constant.10.clone.field_hbm, ...), custom_call_target="tpu_custom_call" | custom-call | tf_op jit(solution)/shard_map/pallas_call | solution.py:506
  81.4 1.9 %shard_map.95 = (f32[3,52,721]{2,1,0:T(8,128)}, f32[52]{0:T(128)}, f32[52]{0:T(128)}) custom-call(f32[1024,128]{1,0:T(8,128)} %shard_map.94.full), custom_call_target="tpu_custom_call" | custom-call | tf_op jit(solution)/shard_map/pallas_call | solution.py:516

commit v5 on v4

--- a/solution.py
+++ b/solution.py
@@ -433,21 +433,31 @@
             back_lon[j, s] = exchange(base + (j - 1) * n_z + s, full.at[mine], full.at[mine], lon_peer(j))
     base += (n_lon - 1) * n_z
     back_core = {}
+    outs = []
+
+    def put_out(index, rows_out):
+        copy = pltpu.make_async_copy(full.at[rows_out], result.at[rows_out], load_sem.at[index])
+        copy.start()
+        outs.append(copy)
+
     for j in (0, *near_first):
         if j > 0:
             for p in range(n_z):
                 back_lon[j, p].wait_recv()
         rows_j = part(core * s_half + quarter(j), s_quart)
         back_core[j] = exchange(base + j, full.at[rows_j], full.at[rows_j], sibling)
-    for c in back_core.values():
+        put_out(j, rows_j)
+    for j, c in back_core.items():
         c.wait_recv()
+        put_out(n_lon + j, part((1 - core) * s_half + quarter(j), s_quart))
     for group in (cross, over_lon, over_z, back_lon, back_core):
         for c in group.values():
             c.wait_send()
     for c in sends.values():
         c.wait_send()
 
-    result[...] = full[...]
+    for c in outs:
+        c.wait()
 
 
 def finish(waves, full, energy, rms, corr):
@@ -507,7 +517,7 @@
         functools.partial(kernel, dims),
         out_shape=jax.ShapeDtypeStruct((size, LANES), f32),
         in_specs=[any_spec] * 7,
-        out_specs=vmem,
+        out_specs=any_spec,
         scratch_shapes=scratch,
         compiler_params=pltpu.CompilerParams(
             collective_id=0, has_side_effects=True, vmem_limit_bytes=60_000_000

time: 83.4 us -> 83 us (level)
  no operation moved by 1% of the time
where the time goes in v5:
time: 83 us; the launch traced here: 82.4 us
  Pallas kernels  81.8 us (99%)
    pallas_call x1, Pallas kernels, fused(): pl.pallas_call(functools.partial(kernel, dims), out_shape=jax.ShapeDtypeS...  79.9 us
    pallas_call x1, Pallas kernels, fused(): pl.pallas_call(functools.partial(finish, waves), out_shape=(jax.ShapeDtyp...  1.87 us

profile of v5, /device:TPU:0, one launch (start us, length us, event | category | flops | bytes accessed | tf_op | source)
XLA Modules:
  0.0 82.4 jit_solution(12283138094181295637)
XLA Ops:
  0.6 79.9 %shard_map.94.full = f32[1024,128]{1,0:T(8,128)} custom-call(f32[360,1664]{1,0:T(8,128)} %fore.1, f32[360,1664]{1,0:T(8,128)} %true.1, f32[360,1664]{1,0:T(8,128)} %norm.1, bf16[4,368,384]{2,1,0:T(8,128)(2,1)} %constant.8.clone.hi_hbm, bf16[4,368,384]{2,1,0:T(8,128)(2,1)} %constant.9.clone.lo_hbm, s32[17,128]{1,0:T(8,128)} %constant.10.clone.field_hbm, ...), custom_call_target="tpu_custom_call" | custom-call | tf_op jit(solution)/shard_map/pallas_call | solution.py:516
  80.6 1.9 %shard_map.95 = (f32[3,52,721]{2,1,0:T(8,128)}, f32[52]{0:T(128)}, f32[52]{0:T(128)}) custom-call(f32[1024,128]{1,0:T(8,128)} %shard_map.94.full), custom_call_target="tpu_custom_call" | custom-call | tf_op jit(solution)/shard_map/pallas_call | solution.py:526
